TPU v7x, 32 devices: a whole 2x2x4 slice. The times are simulated.
32 devices in a mesh: dp: 2 (over x), ctx: 4 (over y, core), tp: 4 (over z).
Axes of the slice: x: 2, y: 2, z: 4, core: 2. Of those that a mesh axis runs over, the one named last changes fastest.
Arguments:
- tokens: bfloat16 [16384, 768], P(('dp', 'ctx', 'tp')), may hold values from -6 to 6
- first_gain: bfloat16 [768], replicated, may hold values from 0.5 to 1.5
- first_bias: bfloat16 [768], replicated, may hold values from -0.4375 to 0.4375
- mixer_weight: bfloat16 [768, 3, 768], P(None, None, 'tp'), may hold values from -0.21875 to 0.21875
- mixer_bias: bfloat16 [3, 768], P(None, 'tp'), may hold values from -0.3125 to 0.3125
- feature_weight: bfloat16 [2, 12, 64, 64], P(None, 'tp'), may hold values from -1.5 to 1.5
- feature_bias: bfloat16 [2, 12, 64], P(None, 'tp'), may hold values from -6 to 6
- output_weight: bfloat16 [768, 768], P('tp'), may hold values from -6 to 6
- output_bias: bfloat16 [768], replicated, may hold values from -4 to 4
- second_gain: bfloat16 [768], replicated, may hold values from 0.5 to 1.5
- second_bias: bfloat16 [768], replicated, may hold values from -4 to 4
- inner_weight: bfloat16 [768, 3072], P(None, 'tp'), may hold values from -0.21875 to 0.21875
- inner_bias: bfloat16 [3072], P('tp'), may hold values from -4 to 4
- outer_weight: bfloat16 [3072, 768], P('tp'), may hold values from -0.109375 to 0.109375
- outer_bias: bfloat16 [768], replicated, may hold values from -4 to 4
- block_owner: int32 [2, 32], P('dp'), may hold values from 0 to 0, as said below
- cotangent: bfloat16 [16384, 768], P(('dp', 'ctx', 'tp')), may hold values from -6 to 6
Outputs:
- result: bfloat16 [16384, 768], P(('dp', 'ctx', 'tp'))
- tokens_gradient: float32 [16384, 768], P(('dp', 'ctx', 'tp'))
- first_gain_gradient: float32 [768], replicated
- first_bias_gradient: float32 [768], replicated
- mixer_weight_gradient: float32 [768, 3, 768], P(None, None, 'tp')
- mixer_bias_gradient: float32 [3, 768], P(None, 'tp')
- feature_weight_gradient: float32 [2, 12, 64, 64], P(None, 'tp')
- feature_bias_gradient: float32 [2, 12, 64], P(None, 'tp')
- output_weight_gradient: float32 [768, 768], P('tp')
- output_bias_gradient: float32 [768], replicated
- second_gain_gradient: float32 [768], replicated
- second_bias_gradient: float32 [768], replicated
- inner_weight_gradient: float32 [768, 3072], P(None, 'tp')
- inner_bias_gradient: float32 [3072], P('tp')
- outer_weight_gradient: float32 [3072, 768], P('tp')
- outer_bias_gradient: float32 [768], replicated
Inputs may be any that keep to these rules, and one draw needn't show every extreme that they name: `block_owner`: all blocks of one sequence carry one number, and pieces of a data group share the same blocks. A sequence covers 8192 // 256 or twice that many consecutive blocks of every piece, so it has 8192 or 16384 tokens; its number is the index of its last 8192-token unit, so numbers rise along a row, differ between sequences, and the last block of every row carries 1 - 1.
All inputs are finite; a program needn't handle non-finite values.
Results may differ from a plain program's by a relative error of at most 0.015.
Values may be sent and summed in bfloat16 or wider, within the bound.
A program may use at most 128 MiB of HBM per device.

v0:
```python
import jax
import jax.numpy as jnp
from jax import lax
from jax.sharding import PartitionSpec as P

HD = 64
BLOCK = 64
SHORT = 8192
EPSILON = 1e-05
HIGHEST = lax.Precision.HIGHEST


def entering(x, axis, combine, identity, reverse):
    peers, mine = (lax.axis_size(axis), lax.axis_index(axis))
    everything = jax.tree.map(lambda part: lax.all_gather(part, axis), x)
    start = jax.tree.map(
        lambda part, zero: jnp.broadcast_to(jnp.asarray(zero, part.dtype), part.shape), x, identity
    )

    def turn(k, before):
        at = peers - 1 - k if reverse else k
        reached = at > mine if reverse else at < mine
        new = combine(before, jax.tree.map(lambda part: part[at], everything))
        return jax.tree.map(lambda a, b: jnp.where(reached, a, b), new, before)

    return lax.fori_loop(0, peers, turn, start)


def layer_norm(values, norm_gain, norm_offset):
    average = jnp.mean(values, axis=-1, keepdims=True)
    centered = values - average
    variance = jnp.mean(centered * centered, axis=-1, keepdims=True)
    return centered * lax.rsqrt(variance + EPSILON) * norm_gain + norm_offset


def gaussian_unit(values):
    return (
        0.5
        * values
        * (1.0 + jnp.tanh(0.7978845608028654 * (values + 0.044715 * values * values * values)))
    )


def feature_map(inputs, weight, offset):
    logits = jnp.einsum("thd,hde->the", inputs, weight, precision=HIGHEST) + offset
    return jnp.concatenate(
        [jax.nn.softmax(logits, axis=-1), jax.nn.softmax(-logits, axis=-1)], axis=-1
    )


def rounded(values):
    return lax.optimization_barrier(values.astype(jnp.bfloat16)).astype(jnp.float32)


def add_pair(first_pair, second_pair):
    return (first_pair[0] + second_pair[0], first_pair[1] + second_pair[1])


def shards(
    tokens,
    first_gain,
    first_bias,
    mixer_weight,
    mixer_bias,
    feature_weight,
    feature_bias,
    output_weight,
    output_bias,
    second_gain,
    second_bias,
    inner_weight,
    inner_bias,
    outer_weight,
    outer_bias,
    block_owner,
    cotangent,
):
    local_rows, model_width = tokens.shape
    heads_here = mixer_weight.shape[2] // HD
    piece_rows = local_rows * lax.axis_size("tp")
    blocks = piece_rows // BLOCK
    unit_count = piece_rows * lax.axis_size("ctx") // SHORT
    owners = block_owner[0]
    block_index = jnp.arange(blocks)
    member = (owners[:, None] == jnp.arange(unit_count)[None, :]).astype(jnp.float32)
    earlier = (
        (owners[:, None] == owners[None, :]) & (block_index[:, None] > block_index[None, :])
    ).astype(jnp.float32)
    causal = jnp.arange(BLOCK)[:, None] >= jnp.arange(BLOCK)[None, :]
    inputs = tokens.astype(jnp.float32)
    first_normed, first_pull = jax.vjp(
        layer_norm, inputs, first_gain.astype(jnp.float32), first_bias.astype(jnp.float32)
    )
    first_low = first_normed.astype(jnp.bfloat16)
    first_rows = lax.all_gather(first_low, "tp", axis=0, tiled=True)
    mixer_flat = mixer_weight.reshape(model_width, -1)
    mixed_rows = jnp.dot(
        first_rows, mixer_flat, preferred_element_type=jnp.float32
    ) + mixer_bias.astype(jnp.float32).reshape(-1)
    mixed_low = mixed_rows.astype(jnp.bfloat16).reshape(piece_rows, 3, heads_here, HD)
    query_rows = mixed_low[:, 0]
    key_rows = mixed_low[:, 1]
    value_rows = mixed_low[:, 2]
    weight_float = feature_weight.astype(jnp.float32)
    bias_float = feature_bias.astype(jnp.float32)
    query_lifted, query_pull = jax.vjp(
        feature_map, query_rows.astype(jnp.float32), weight_float[0], bias_float[0]
    )
    key_lifted, key_pull = jax.vjp(
        feature_map, key_rows.astype(jnp.float32), weight_float[1], bias_float[1]
    )
    query_blocks = query_lifted.astype(jnp.bfloat16).reshape(blocks, BLOCK, heads_here, 2 * HD)
    key_blocks = key_lifted.astype(jnp.bfloat16).reshape(blocks, BLOCK, heads_here, 2 * HD)
    value_blocks = value_rows.reshape(blocks, BLOCK, heads_here, HD)
    block_state = jnp.einsum(
        "jthe,jthf->jhef", value_blocks, key_blocks, preferred_element_type=jnp.float32
    )
    block_norm = jnp.sum(key_blocks.astype(jnp.float32), axis=1)
    totals = (
        jnp.einsum("js,jhef->shef", member, block_state, precision=HIGHEST),
        jnp.einsum("js,jhf->shf", member, block_norm, precision=HIGHEST),
    )
    incoming = entering(
        (totals[0], totals[1]),
        "ctx",
        add_pair,
        (jnp.zeros_like(totals[0]), jnp.zeros_like(totals[1])),
        False,
    )
    state_before = jnp.einsum(
        "ji,ihef->jhef", earlier, block_state, precision=HIGHEST
    ) + jnp.einsum("js,shef->jhef", member, incoming[0], precision=HIGHEST)
    norm_before = jnp.einsum("ji,ihf->jhf", earlier, block_norm, precision=HIGHEST) + jnp.einsum(
        "js,shf->jhf", member, incoming[1], precision=HIGHEST
    )
    numerator = jnp.einsum(
        "jthf,jhef->jthe",
        query_blocks,
        state_before,
        precision=HIGHEST,
        preferred_element_type=jnp.float32,
    )
    denominator = jnp.einsum(
        "jthf,jhf->jth",
        query_blocks,
        norm_before,
        precision=HIGHEST,
        preferred_element_type=jnp.float32,
    )
    scores = jnp.einsum(
        "jthf,jshf->jhts", query_blocks, key_blocks, preferred_element_type=jnp.float32
    )
    scores_low = jnp.where(causal, scores, 0.0).astype(jnp.bfloat16)
    numerator = numerator + jnp.einsum(
        "jhts,jshe->jthe", scores_low, value_blocks, preferred_element_type=jnp.float32
    )
    denominator = denominator + jnp.swapaxes(jnp.sum(scores_low.astype(jnp.float32), axis=-1), 1, 2)
    attended = numerator / denominator[..., None]
    attended_low = attended.astype(jnp.bfloat16).reshape(piece_rows, heads_here * HD)
    attention_sum = lax.psum_scatter(
        jnp.dot(attended_low, output_weight, preferred_element_type=jnp.float32),
        "tp",
        scatter_dimension=0,
        tiled=True,
    )
    middle = inputs + attention_sum + output_bias.astype(jnp.float32)
    second_normed, second_pull = jax.vjp(
        layer_norm, middle, second_gain.astype(jnp.float32), second_bias.astype(jnp.float32)
    )
    second_low = second_normed.astype(jnp.bfloat16)
    second_rows = lax.all_gather(second_low, "tp", axis=0, tiled=True)
    hidden_input = jnp.dot(
        second_rows, inner_weight, preferred_element_type=jnp.float32
    ) + inner_bias.astype(jnp.float32)
    activated_float, curve_pull = jax.vjp(gaussian_unit, hidden_input)
    activated = activated_float.astype(jnp.bfloat16)
    branch_out = lax.psum_scatter(
        jnp.dot(activated, outer_weight, preferred_element_type=jnp.float32).astype(jnp.bfloat16),
        "tp",
        scatter_dimension=0,
        tiled=True,
    ).astype(jnp.float32)
    result = (middle + branch_out + outer_bias.astype(jnp.float32)).astype(jnp.bfloat16)
    upstream = cotangent.astype(jnp.float32)
    upstream_rows = lax.all_gather(cotangent, "tp", axis=0, tiled=True)
    outer_delta = jnp.einsum(
        "tf,td->fd", activated, upstream_rows, preferred_element_type=jnp.float32
    )
    activated_delta = jnp.einsum(
        "td,fd->tf", upstream_rows, outer_weight, preferred_element_type=jnp.float32
    )
    (hidden_delta,) = curve_pull(activated_delta)
    hidden_low = hidden_delta.astype(jnp.bfloat16)
    inner_bias_delta = jnp.sum(hidden_low.astype(jnp.float32), axis=0)
    inner_delta = jnp.einsum(
        "td,tf->df", second_rows, hidden_low, preferred_element_type=jnp.float32
    )
    second_delta = lax.psum_scatter(
        jnp.einsum("tf,df->td", hidden_low, inner_weight, preferred_element_type=jnp.float32),
        "tp",
        scatter_dimension=0,
        tiled=True,
    )
    middle_back, second_gain_part, second_bias_part = second_pull(second_delta)
    middle_delta = upstream + middle_back
    middle_low = middle_delta.astype(jnp.bfloat16)
    middle_rows = lax.all_gather(middle_low, "tp", axis=0, tiled=True)
    output_delta = jnp.einsum(
        "tk,td->kd", attended_low, middle_rows, preferred_element_type=jnp.float32
    )
    attended_delta = rounded(
        jnp.einsum("td,kd->tk", middle_rows, output_weight, preferred_element_type=jnp.float32)
    )
    attended_delta = attended_delta.reshape(blocks, BLOCK, heads_here, HD)
    numerator_delta = attended_delta / denominator[..., None]
    denominator_delta = -jnp.sum(attended_delta * attended, axis=-1) / denominator
    score_delta = (
        jnp.einsum(
            "jthe,jshe->jhts",
            numerator_delta,
            value_blocks,
            precision=HIGHEST,
            preferred_element_type=jnp.float32,
        )
        + jnp.swapaxes(denominator_delta, 1, 2)[..., None]
    )
    score_low = jnp.where(causal, score_delta, 0.0).astype(jnp.bfloat16)
    value_delta = jnp.einsum(
        "jhts,jthe->jshe",
        scores_low,
        numerator_delta,
        precision=HIGHEST,
        preferred_element_type=jnp.float32,
    )
    query_delta = (
        jnp.einsum("jhts,jshf->jthf", score_low, key_blocks, preferred_element_type=jnp.float32)
        + jnp.einsum(
            "jthe,jhef->jthf",
            numerator_delta,
            state_before,
            precision=HIGHEST,
            preferred_element_type=jnp.float32,
        )
        + denominator_delta[..., None] * norm_before[:, None]
    )
    key_delta = jnp.einsum(
        "jhts,jthf->jshf", score_low, query_blocks, preferred_element_type=jnp.float32
    )
    before_delta = jnp.einsum(
        "jthf,jthe->jhef",
        query_blocks,
        numerator_delta,
        precision=HIGHEST,
        preferred_element_type=jnp.float32,
    )
    norm_before_delta = jnp.einsum(
        "jthf,jth->jhf",
        query_blocks,
        denominator_delta,
        precision=HIGHEST,
        preferred_element_type=jnp.float32,
    )
    leaving = (
        jnp.einsum("js,jhef->shef", member, before_delta, precision=HIGHEST),
        jnp.einsum("js,jhf->shf", member, norm_before_delta, precision=HIGHEST),
    )
    later_sums = entering(
        (leaving[0], leaving[1]),
        "ctx",
        add_pair,
        (jnp.zeros_like(leaving[0]), jnp.zeros_like(leaving[1])),
        True,
    )
    state_delta = jnp.einsum(
        "ji,jhef->ihef", earlier, before_delta, precision=HIGHEST
    ) + jnp.einsum("js,shef->jhef", member, later_sums[0], precision=HIGHEST)
    block_norm_delta = jnp.einsum(
        "ji,jhf->ihf", earlier, norm_before_delta, precision=HIGHEST
    ) + jnp.einsum("js,shf->jhf", member, later_sums[1], precision=HIGHEST)
    value_delta = value_delta + jnp.einsum(
        "jhef,jthf->jthe",
        state_delta,
        key_blocks,
        precision=HIGHEST,
        preferred_element_type=jnp.float32,
    )
    key_delta = (
        key_delta
        + jnp.einsum(
            "jhef,jthe->jthf",
            state_delta,
            value_blocks,
            precision=HIGHEST,
            preferred_element_type=jnp.float32,
        )
        + block_norm_delta[:, None]
    )
    query_in_delta, query_weight_delta, query_bias_delta = query_pull(
        rounded(query_delta).reshape(piece_rows, heads_here, 2 * HD)
    )
    key_in_delta, key_weight_delta, key_bias_delta = key_pull(
        rounded(key_delta).reshape(piece_rows, heads_here, 2 * HD)
    )
    mixed_delta = jnp.stack(
        [query_in_delta, key_in_delta, value_delta.reshape(piece_rows, heads_here, HD)], axis=1
    )
    mixed_delta = mixed_delta.astype(jnp.bfloat16).reshape(piece_rows, 3 * heads_here * HD)
    mixer_bias_delta = jnp.sum(mixed_delta.astype(jnp.float32), axis=0).reshape(3, heads_here * HD)
    mixer_delta = jnp.einsum(
        "td,tk->dk", first_rows, mixed_delta, preferred_element_type=jnp.float32
    ).reshape(model_width, 3, heads_here * HD)
    first_delta = lax.psum_scatter(
        jnp.einsum("tk,dk->td", mixed_delta, mixer_flat, preferred_element_type=jnp.float32).astype(
            jnp.bfloat16
        ),
        "tp",
        scatter_dimension=0,
        tiled=True,
    ).astype(jnp.float32)
    input_back, first_gain_part, first_bias_part = first_pull(first_delta)
    tokens_delta = middle_delta + input_back
    feature_weight_delta = jnp.stack([query_weight_delta, key_weight_delta])
    feature_bias_delta = jnp.stack([query_bias_delta, key_bias_delta])
    output_bias_part = jnp.sum(middle_delta, axis=0)
    outer_bias_part = jnp.sum(upstream, axis=0)
    summed = lax.psum(
        (
            mixer_delta,
            mixer_bias_delta,
            feature_weight_delta,
            feature_bias_delta,
            output_delta,
            inner_delta,
            inner_bias_delta,
            outer_delta,
            first_gain_part,
            first_bias_part,
            output_bias_part,
            second_gain_part,
            second_bias_part,
            outer_bias_part,
        ),
        ("dp", "ctx"),
    )
    shared = lax.psum((summed[8], summed[9], summed[10], summed[11], summed[12], summed[13]), "tp")
    return (
        result,
        tokens_delta,
        shared[0],
        shared[1],
        summed[0],
        summed[1],
        summed[2],
        summed[3],
        summed[4],
        shared[2],
        shared[3],
        shared[4],
        summed[5],
        summed[6],
        summed[7],
        shared[5],
    )


def solution(mesh):
    in_specs = (
        P(("dp", "ctx", "tp"), None),
        P(),
        P(),
        P(None, None, "tp"),
        P(None, "tp"),
        P(None, "tp", None, None),
        P(None, "tp", None),
        P("tp", None),
        P(),
        P(),
        P(),
        P(None, "tp"),
        P("tp"),
        P("tp", None),
        P(),
        P("dp", None),
        P(("dp", "ctx", "tp"), None),
    )
    out_specs = (
        P(("dp", "ctx", "tp"), None),
        P(("dp", "ctx", "tp"), None),
        P(),
        P(),
        P(None, None, "tp"),
        P(None, "tp"),
        P(None, "tp", None, None),
        P(None, "tp", None),
        P("tp", None),
        P(),
        P(),
        P(),
        P(None, "tp"),
        P("tp"),
        P("tp", None),
        P(),
    )
    return jax.shard_map(shards, mesh=mesh, in_specs=in_specs, out_specs=out_specs, check_vma=False)
```

profile of v0, /device:TPU:0, one launch (start us, length us, event | category | flops | bytes accessed | tf_op | source)
XLA Modules:
  0.0 1006.3 jit_solution(10132067115701984201)
XLA Ops:
  14.2 65.0 %all-gather.11.cloned.1.call-done = bf16[2048,768]{1,0:T(8,128)(2,1)} async-done(((bf16[512,768]{1,0:T(8,128)(2,1)}), bf16[2048,768]{1,0:T(8,128)(2,1)}) %all-gather.11.cloned.1.call-update) | async-done | bytes 3145744 | tf_op jit(solution)/shard_map/all_gather | solution.py:95
  79.2 3.9 add_convert_fusion
  94.4 3.4 reshape_squeeze.3
  97.8 3.4 copy.124
  103.5 3.4 concatenate.19
  117.1 4.3 convert_reduce_fusion.3
  121.6 5.6 all-gather.4
  129.9 3.5 copy.115
  135.1 3.4 concatenate.21
  138.5 3.5 copy.114
  147.0 7.0 all-gather
  154.0 6.5 while.34
  161.7 5.7 multiply_add_fusion.3
  171.9 4.7 fusion.25
  184.6 3.7 fusion.127
  189.6 108.3 %reduce-scatter.5.cloned.1.call-done = f32[512,768]{1,0:T(8,128)} async-done(((f32[2048,768]{1,0:T(8,128)}), f32[512,768]{1,0:T(8,128)}) %reduce-scatter.5.cloned.1.call-update) | async-done | bytes 1572880 | tf_op jit(solution)/shard_map/reduce_scatter | solution.py:160
  303.6 62.3 %all-gather.13.cloned.1.call-done = bf16[2048,768]{1,0:T(8,128)(2,1)} async-done(((bf16[512,768]{1,0:T(8,128)(2,1)}), bf16[2048,768]{1,0:T(8,128)(2,1)}) %all-gather.13.cloned.1.call-update) | async-done | bytes 3145744 | tf_op jit(solution)/shard_map/all_gather | solution.py:171
  365.9 7.5 fusion.128
  373.4 56.1 %all-gather.15.cloned.1.call-done = bf16[2048,768]{1,0:T(8,128)(2,1)} async-done(((bf16[512,768]{1,0:T(8,128)(2,1)}), bf16[2048,768]{1,0:T(8,128)(2,1)}) %all-gather.15.cloned.1.call-update) | async-done | bytes 3145744 | tf_op jit(solution)/shard_map/all_gather | solution.py:185
  429.5 12.2 %convert_reduce_fusion = (f32[768]{0:T(1024)}, bf16[2048,768]{1,0:T(8,128)(2,1)S(1)}, bf16[2048,768]{1,0:T(8,128)(2,1)}) fusion(f32[2048,768]{1,0:T(8,128)} %fusion.128, f32[768]{0:T(1024)} %convert_element_type.136, bf16[2048,768]{1,0:T(8,128)(2,1)} %all-gather.15.cloned.1.call-done, bf16[768,768]{1,0:T(8,128)(2,1)S(1)} %copy-done), kind=kOutput, calls=%fused_computation.18 | convolution fusion | flops 2461531392 | bytes 16914432 | tf_op jit(solution)/shard_map/td,fd->tf/dot_general | solution.py:189
  443.4 4.6 fusion.129
  448.1 6.3 convolution_convert_fusion
  455.0 102.6 %reduce-scatter.9.cloned.1.call-done = f32[512,768]{1,0:T(8,128)} async-done(((f32[2048,768]{1,0:T(8,128)}), f32[512,768]{1,0:T(8,128)}) %reduce-scatter.9.cloned.1.call-update) | async-done | bytes 1572880 | tf_op jit(solution)/shard_map/reduce_scatter | solution.py:198
  560.2 60.3 %reduce-scatter.7.cloned.1.call-done = bf16[512,768]{1,0:T(8,128)(2,1)} async-done(((bf16[2048,768]{1,0:T(8,128)(2,1)}), bf16[512,768]{1,0:T(8,128)(2,1)}) %reduce-scatter.7.cloned.1.call-update) | async-done | bytes 786448 | tf_op jit(solution)/shard_map/reduce_scatter | solution.py:177
  629.5 60.4 %all-gather.17.cloned.1.call-done = bf16[2048,768]{1,0:T(8,128)(2,1)} async-done(((bf16[512,768]{1,0:T(8,128)(2,1)}), bf16[2048,768]{1,0:T(8,128)(2,1)}) %all-gather.17.cloned.1.call-update) | async-done | bytes 3145744 | tf_op jit(solution)/shard_map/all_gather | solution.py:207
  695.6 5.2 multiply_reduce_fusion
  701.0 10.8 %fusion.23 = f32[32,3,128,64]{2,3,1,0:T(8,128)} fusion(f32[32,3,64,128]{3,0,2,1:T(8,128)S(1)} %copy-done.27, f32[32,64,3,64]{1,0,3,2:T(8,128)S(1)} %copy-done.24, f32[32,64,3]{1,2,0:T(4,128)S(1)} %copy-done.56), kind=kOutput, calls=%fused_computation.50 | convolution fusion | flops 604372992 | bytes 7888896 | tf_op jit(solution)/shard_map/jthe,jhef->jthf/dot_general | solution.py:237
  711.8 4.3 fusion.111
  717.6 5.2 all-gather.5
  725.7 6.5 all-gather.2
  733.0 5.7 multiply_add_fusion.2
  738.7 4.8 fusion.15
  743.6 4.5 fusion.17
  748.1 4.4 select_convert_fusion
  756.5 4.9 bitcast_add_fusion
  767.2 3.7 fusion.119
  770.9 3.4 copy.180
  776.1 3.4 copy.181
  781.8 3.6 fusion.118
  790.9 3.6 copy.179
  797.4 4.9 fusion.113
  806.1 4.1 convolution_convert_fusion.1
  810.5 7.0 fusion.132
  817.5 4.1 fusion.131
  830.0 39.3 %reduce-scatter.11.cloned.1.call-done = bf16[512,768]{1,0:T(8,128)(2,1)} async-done(((bf16[2048,768]{1,0:T(8,128)(2,1)}), bf16[512,768]{1,0:T(8,128)(2,1)}) %reduce-scatter.11.cloned.1.call-update) | async-done | bytes 786448 | tf_op jit(solution)/shard_map/reduce_scatter | solution.py:312
  875.3 26.5 %all-reduce = (f32[768]{0:T(1024)S(1)}, f32[768]{0:T(1024)S(1)}, f32[3,192]{1,0:T(4,128)}, f32[2,3,64]{2,1,0:T(4,128)S(1)}, f32[768]{0:T(1024)S(1)}, /*index=5*/...) all-reduce(f32[768]{0:T(1024)S(1)} %get-tuple-element.373, ...), channel_id=1, replica_groups=mesh['dp'=2,'ctx'=4,'tp'=4] {'dp','ctx'}, use_global_device_ids=true, to_apply=%region_32.33 | all-reduce | flops 6336 | bytes 50688 | tf_op jit(solution)/shard_map/psum | solution.py:326
  902.4 18.5 %all-reduce.2 = (f32[768]{0:T(1024)}, f32[768]{0:T(1024)}, f32[768]{0:T(1024)}, f32[768]{0:T(1024)}, f32[768]{0:T(1024)}, /*index=5*/f32[768]{0:T(1024)}) all-reduce(f32[768]{0:T(1024)S(1)} %get-tuple-element.404, f32[768]{0:T(1024)S(1)} %get-tuple-element.405, ...), channel_id=1, replica_groups=mesh['dp'=2,'ctx'=4,'tp'=4] {'tp'}, use_global_device_ids=true, to_apply=%region_33.34 | all-reduce | flops 4608 | bytes 36864 | tf_op jit(solution)/shard_map/psum | solution.py:345
  920.9 70.3 %all-reduce.5.cloned.1.call-done = (f32[768,3,192]{0,2,1:T(8,128)}, f32[2,3,64,64]{3,2,1,0:T(8,128)}, f32[192,768]{1,0:T(8,128)}, f32[768,768]{1,0:T(8,128)}, f32[768,768]{1,0:T(8,128)}) async-done(((f32[768,3,192]{0,2,1:T(8,128)}, f32[2,3,64,64]{3,2,1,0:T(8,128)}, f32[192,768]{1,0:T(8,128)}, f32[768,768]{1,0:T(8,128)}, f32[768,768]{1,0:T(8,128)}), (f32[768,3,192]{0,2,1:T(8,128)}, ...) | async-done | bytes 7176208 | tf_op jit(solution)/shard_map/psum | solution.py:326
  (353 shorter events, 141.3 us)
Async XLA Ops:
  7.2 422.3 %copy-start = (bf16[768,768]{1,0:T(8,128)(2,1)S(1)}, bf16[768,768]{1,0:T(8,128)(2,1)}, u32[]{:S(2)}) copy-start(bf16[768,768]{1,0:T(8,128)(2,1)} %param.34) | copy-start | bytes 3538948
  7.2 72.0 %all-gather.11.cloned.1.call-start = ((), (), s32[]{:S(2)}) async-start(), calls=%async_computation.4 | async-start | bytes 3932160 | tf_op jit(solution)/shard_map/all_gather | solution.py:95
  8.8 4.9 copy-start.75
  8.8 70.4 %copy-start.98 = (bf16[768,3,192]{0,2,1:T(8,128)(2,1)S(1)}, bf16[768,3,192]{0,2,1:T(8,128)(2,1)}, u32[]{:S(2)}) copy-start(bf16[768,3,192]{0,2,1:T(8,128)(2,1)} %param.24) | copy-start | bytes 2654212
  12.8 285.1 %reduce-scatter.5.cloned.1.call-start = ((), (), s32[]{:S(2)}) async-start(), calls=%async_computation.5 | async-start | bytes 7864320 | tf_op jit(solution)/shard_map/reduce_scatter | solution.py:160
  83.1 6.6 copy-start.34
  87.5 22.8 %copy-start.5 = (f32[2048,3,64]{0,2,1:T(8,128)}, f32[2048,3,64]{0,2,1:T(8,128)S(1)}, u32[]{:S(2)}) copy-start(f32[2048,3,64]{0,2,1:T(8,128)S(1)} %get-tuple-element.454) | copy-start | bytes 4718596
  117.1 10.1 %copy-start.11 = (f32[2048,3,64]{0,2,1:T(8,128)S(1)}, f32[2048,3,64]{0,2,1:T(8,128)}, u32[]{:S(2)}) copy-start(f32[2048,3,64]{0,2,1:T(8,128)} %get-tuple-element.448) | copy-start | bytes 4718596
  117.1 10.1 %copy-start.48 = (f32[2048,3]{0,1:T(4,128)S(1)}, f32[2048,3]{0,1:T(4,128)}, u32[]{:S(2)}) copy-start(f32[2048,3]{0,1:T(4,128)} %get-tuple-element.447) | copy-start | bytes 73732
  121.4 5.8 copy-start.59
  161.7 7.7 copy-start.71
  161.7 5.7 copy-start.36
  161.7 5.7 copy-start.37
  169.3 7.3 copy-start.57
  169.4 7.3 copy-start.100
  171.9 4.7 copy-start.61
  171.9 4.8 copy-start.20
  188.3 177.6 %all-gather.13.cloned.1.call-start = ((), (), s32[]{:S(2)}) async-start(), calls=%async_computation.6 | async-start | bytes 3932160 | tf_op jit(solution)/shard_map/all_gather | solution.py:171
  301.7 127.8 %all-gather.15.cloned.1.call-start = ((), (), s32[]{:S(2)}) async-start(), calls=%async_computation.8 | async-start | bytes 3932160 | tf_op jit(solution)/shard_map/all_gather | solution.py:185
  302.3 255.3 %reduce-scatter.9.cloned.1.call-start = ((), (), s32[]{:S(2)}) async-start(), calls=%async_computation.9 | async-start | bytes 7864320 | tf_op jit(solution)/shard_map/reduce_scatter | solution.py:198
  429.5 13.9 %copy-start.97 = (bf16[768,768]{1,0:T(8,128)(2,1)S(1)}, bf16[768,768]{1,0:T(8,128)(2,1)}, u32[]{:S(2)}) copy-start(bf16[768,768]{1,0:T(8,128)(2,1)} %param.32) | copy-start | bytes 3538948
  448.0 172.5 %reduce-scatter.7.cloned.1.call-start = ((), (), s32[]{:S(2)}) async-start(), calls=%async_computation.7 | async-start | bytes 3932160 | tf_op jit(solution)/shard_map/reduce_scatter | solution.py:177
  454.4 235.5 %all-gather.17.cloned.1.call-start = ((), (), s32[]{:S(2)}) async-start(), calls=%async_computation.10 | async-start | bytes 3932160 | tf_op jit(solution)/shard_map/all_gather | solution.py:207
  455.0 105.2 %copy-start.79 = (f32[512]{0:T(512)S(1)}, f32[512]{0:T(512)}, u32[]{:S(2)}) copy-start(f32[512]{0:T(512)} %copy-done.78) | copy-start | bytes 6148
  560.2 64.8 %copy-start.32 = (bf16[512,768]{1,0:T(8,128)(2,1)S(1)}, bf16[512,768]{1,0:T(8,128)(2,1)}, u32[]{:S(2)}) copy-start(bf16[512,768]{1,0:T(8,128)(2,1)} %param.37) | copy-start | bytes 2359300
  625.0 64.9 %copy-start.53 = (bf16[192,768]{1,0:T(8,128)(2,1)S(1)}, bf16[192,768]{1,0:T(8,128)(2,1)}, u32[]{:S(2)}) copy-start(bf16[192,768]{1,0:T(8,128)(2,1)} %param.28) | copy-start | bytes 884740
  626.2 243.1 %reduce-scatter.11.cloned.1.call-start = ((), (), s32[]{:S(2)}) async-start(), calls=%async_computation.11 | async-start | bytes 3932160 | tf_op jit(solution)/shard_map/reduce_scatter | solution.py:312
  692.9 7.9 copy-start.58
  693.0 7.9 copy-start.62
  695.6 5.3 copy-start.56
  695.6 5.4 copy-start.24
  695.6 5.4 copy-start.27
  701.0 10.8 %copy-start.23 = (bf16[32,64,3,128]{3,1,2,0:T(8,128)(2,1)S(1)}, bf16[32,64,3,128]{3,1,2,0:T(8,128)(2,1)}, u32[]{:S(2)}) copy-start(bf16[32,64,3,128]{3,1,2,0:T(8,128)(2,1)} %copy-done.22) | copy-start | bytes 4718596
  716.1 9.5 copy-start.28
  725.7 7.3 copy-start.87
  733.0 5.7 copy-start.13
  738.7 4.8 copy-start.21
  743.5 4.5 copy-start.25
  797.4 4.9 copy-start.51
  810.2 181.0 %all-reduce.5.cloned.1.call-start = ((), (), s32[]{:S(2)}) async-start(), calls=%async_computation.12 | async-start | bytes 14548992 | tf_op jit(solution)/shard_map/psum | solution.py:326
  810.5 7.1 copy-start.96
  810.5 7.1 copy-start.103
  817.5 7.2 copy-start.38
  829.8 39.5 %copy-start.68 = (f32[768]{0:T(1024)S(1)}, f32[768]{0:T(1024)}, u32[]{:S(2)}) copy-start(f32[768]{0:T(1024)} %copy-done.67) | copy-start | bytes 9220
  829.8 39.5 %copy-start.70 = (f32[512]{0:T(512)S(1)}, f32[512]{0:T(512)}, u32[]{:S(2)}) copy-start(f32[512]{0:T(512)} %copy-done.69) | copy-start | bytes 6148
  829.9 41.3 %copy-start.77 = (f32[512]{0:T(512)S(1)}, f32[512]{0:T(512)}, u32[]{:S(2)}) copy-start(f32[512]{0:T(512)} %copy-done.76) | copy-start | bytes 6148
  829.9 41.3 %copy-start.74 = (f32[512]{0:T(512)S(1)}, f32[512]{0:T(512)}, u32[]{:S(2)}) copy-start(f32[512]{0:T(512)} %copy-done.73) | copy-start | bytes 6148
  830.0 43.3 %copy-start.19 = (f32[512,768]{1,0:T(8,128)S(1)}, f32[512,768]{1,0:T(8,128)}, u32[]{:S(2)}) copy-start(f32[512,768]{1,0:T(8,128)} %copy-done.18) | copy-start | bytes 4718596
  (65 other events, 172.5 us)
Sparse Core Ops, SparseCore 0:
  12.9 66.1 all-gather.10
  188.4 109.4 reduce-scatter.4
  301.8 64.0 all-gather.12
  367.3 62.1 all-gather.14
  448.2 109.3 reduce-scatter.8
  559.8 60.7 reduce-scatter.6
  626.3 63.5 all-gather.16
  810.4 58.9 reduce-scatter.10
  874.4 116.7 all-reduce.4
where the time goes:
time: 1020 us; the launch traced here: 1010 us
  waiting for transfers between devices  625 us (61%)
  matrix products  136 us (13%)
  local copies, waits for them, and re-layouts  86.1 us (8%)
  other arithmetic  72.6 us (7%)
  blocking collectives  69.3 us (7%)
  between operations  15.4 us (2%)
    reduce_scatter x1, waiting for transfers between devices, shards(): lax.psum_scatter(jnp.dot(attended_low, output_weight, preferred_element_t...  108 us
    reduce_scatter x1, waiting for transfers between devices, shards(): lax.psum_scatter(jnp.einsum('tf,df->td', hidden_low, inner_weight, prefer...  103 us
    psum x1, waiting for transfers between devices, shards(): lax.psum((mixer_delta, mixer_bias_delta, feature_weight_delta, feature_bi...  70.3 us
    all_gather x1, waiting for transfers between devices, shards(): first_rows = lax.all_gather(first_low, 'tp', axis=0, tiled=True)  65 us
    all_gather x1, waiting for transfers between devices, shards(): second_rows = lax.all_gather(second_low, 'tp', axis=0, tiled=True)  62.3 us
    all_gather x1, waiting for transfers between devices, shards(): middle_rows = lax.all_gather(middle_low, 'tp', axis=0, tiled=True)  60.4 us
    reduce_scatter x1, waiting for transfers between devices, shards(): lax.psum_scatter(jnp.dot(activated, outer_weight, preferred_element_type=...  60.3 us
    all_gather x1, waiting for transfers between devices, shards(): upstream_rows = lax.all_gather(cotangent, 'tp', axis=0, tiled=True)  56.1 us
  transfers between devices with their start and end apart: 9, of which 9 were waited for; matrix products, arithmetic and copies ran while one was open for 5% of the time, Pallas kernels for 0%

commit v1 on v0

--- a/solution.py
+++ b/solution.py
@@ -324,23 +324,26 @@
     output_bias_part = jnp.sum(middle_delta, axis=0)
     outer_bias_part = jnp.sum(upstream, axis=0)
     summed = lax.psum(
-        (
-            mixer_delta,
-            mixer_bias_delta,
-            feature_weight_delta,
-            feature_bias_delta,
-            output_delta,
-            inner_delta,
-            inner_bias_delta,
-            outer_delta,
-            first_gain_part,
-            first_bias_part,
-            output_bias_part,
-            second_gain_part,
-            second_bias_part,
-            outer_bias_part,
+        lax.psum(
+            (
+                mixer_delta,
+                mixer_bias_delta,
+                feature_weight_delta,
+                feature_bias_delta,
+                output_delta,
+                inner_delta,
+                inner_bias_delta,
+                outer_delta,
+                first_gain_part,
+                first_bias_part,
+                output_bias_part,
+                second_gain_part,
+                second_bias_part,
+                outer_bias_part,
+            ),
+            "ctx",
         ),
-        ("dp", "ctx"),
+        "dp",
     )
     shared = lax.psum((summed[8], summed[9], summed[10], summed[11], summed[12], summed[13]), "tp")
     return (

time: 1020 us -> 1220 us (1.20)
  waiting for transfers between devices: 625 us -> 828 us
    psum x0 -> x1, waiting for transfers between devices: none -> 133 us  [shards(): lax.psum(lax.psum((mixer_delta, mixer_bias_delta, feature_weight_delta, f...]
    psum x1, waiting for transfers between devices: 70.3 us -> 128 us  [shards(): lax.psum((mixer_delta, mixer_bias_delta, feature_weight_delta, feature_bi...]
    reduce_scatter x1, waiting for transfers between devices: 39.3 us -> 62.8 us  [shards(): lax.psum_scatter(jnp.einsum('tk,dk->td', mixed_delta, mixer_flat, preferr...]
    psum x1, blocking collectives: 26.5 us -> 11.9 us  [shards(): lax.psum((mixer_delta, mixer_bias_delta, feature_weight_delta, feature_bi...]
    unnamed x220 -> x214, local copies, waits for them, and re-layouts: 31.8 us -> 32.7 us
  transfers between devices with their start and end apart: 9 -> 10, of which waited for: 9 -> 10; matrix products, arithmetic and copies ran while one was open for 5% -> 4% of each run, Pallas kernels for 0% -> 0%
where the time goes in v1:
time: 1220 us; the launch traced here: 1210 us
  waiting for transfers between devices  828 us (68%)
  matrix products  141 us (12%)
  local copies, waits for them, and re-layouts  86.3 us (7%)
  other arithmetic  74.4 us (6%)
  blocking collectives  64.6 us (5%)
  between operations  15.6 us (1%)
    psum x1, waiting for transfers between devices, shards(): lax.psum(lax.psum((mixer_delta, mixer_bias_delta, feature_weight_delta, f...  133 us
    psum x1, waiting for transfers between devices, shards(): lax.psum((mixer_delta, mixer_bias_delta, feature_weight_delta, feature_bi...  128 us
    reduce_scatter x1, waiting for transfers between devices, shards(): lax.psum_scatter(jnp.dot(attended_low, output_weight, preferred_element_t...  108 us
    reduce_scatter x1, waiting for transfers between devices, shards(): lax.psum_scatter(jnp.einsum('tf,df->td', hidden_low, inner_weight, prefer...  102 us
    all_gather x1, waiting for transfers between devices, shards(): first_rows = lax.all_gather(first_low, 'tp', axis=0, tiled=True)  65 us
    reduce_scatter x1, waiting for transfers between devices, shards(): lax.psum_scatter(jnp.einsum('tk,dk->td', mixed_delta, mixer_flat, preferr...  62.8 us
    all_gather x1, waiting for transfers between devices, shards(): second_rows = lax.all_gather(second_low, 'tp', axis=0, tiled=True)  62.3 us
    reduce_scatter x1, waiting for transfers between devices, shards(): lax.psum_scatter(jnp.dot(activated, outer_weight, preferred_element_type=...  60.3 us
  transfers between devices with their start and end apart: 10, of which 10 were waited for; matrix products, arithmetic and copies ran while one was open for 4% of the time, Pallas kernels for 0%

profile of v1, /device:TPU:0, one launch (start us, length us, event | category | flops | bytes accessed | tf_op | source)
XLA Modules:
  0.0 1210.2 jit_solution(12297158764987863730)
XLA Ops:
  14.2 65.0 %all-gather.11.cloned.1.call-done = bf16[2048,768]{1,0:T(8,128)(2,1)} async-done(((bf16[512,768]{1,0:T(8,128)(2,1)}), bf16[2048,768]{1,0:T(8,128)(2,1)}) %all-gather.11.cloned.1.call-update) | async-done | bytes 3145744 | tf_op jit(solution)/shard_map/all_gather | solution.py:95
  79.2 3.9 add_convert_fusion
  94.3 3.4 reshape_squeeze.3
  103.5 3.4 concatenate.19
  117.1 4.3 convert_reduce_fusion.3
  121.5 5.3 all-gather.4
  129.5 3.5 copy.115
  134.8 3.4 concatenate.21
  138.2 3.5 copy.114
  146.7 7.0 all-gather
  153.7 6.6 while.34
  161.4 5.7 multiply_add_fusion.3
  171.6 4.7 fusion.25
  184.3 3.7 fusion.127
  189.3 108.3 %reduce-scatter.5.cloned.1.call-done = f32[512,768]{1,0:T(8,128)} async-done(((f32[2048,768]{1,0:T(8,128)}), f32[512,768]{1,0:T(8,128)}) %reduce-scatter.5.cloned.1.call-update) | async-done | bytes 1572880 | tf_op jit(solution)/shard_map/reduce_scatter | solution.py:160
  303.3 62.3 %all-gather.13.cloned.1.call-done = bf16[2048,768]{1,0:T(8,128)(2,1)} async-done(((bf16[512,768]{1,0:T(8,128)(2,1)}), bf16[2048,768]{1,0:T(8,128)(2,1)}) %all-gather.13.cloned.1.call-update) | async-done | bytes 3145744 | tf_op jit(solution)/shard_map/all_gather | solution.py:171
  365.6 7.5 fusion.128
  373.1 56.1 %all-gather.15.cloned.1.call-done = bf16[2048,768]{1,0:T(8,128)(2,1)} async-done(((bf16[512,768]{1,0:T(8,128)(2,1)}), bf16[2048,768]{1,0:T(8,128)(2,1)}) %all-gather.15.cloned.1.call-update) | async-done | bytes 3145744 | tf_op jit(solution)/shard_map/all_gather | solution.py:185
  429.2 12.3 %convert_reduce_fusion = (f32[768]{0:T(1024)}, bf16[2048,768]{1,0:T(8,128)(2,1)S(1)}, bf16[2048,768]{1,0:T(8,128)(2,1)}) fusion(f32[2048,768]{1,0:T(8,128)} %fusion.128, f32[768]{0:T(1024)} %convert_element_type.136, bf16[2048,768]{1,0:T(8,128)(2,1)} %all-gather.15.cloned.1.call-done, bf16[768,768]{1,0:T(8,128)(2,1)S(1)} %copy-done), kind=kOutput, calls=%fused_computation.18 | convolution fusion | flops 2461531392 | bytes 16914432 | tf_op jit(solution)/shard_map/td,fd->tf/dot_general | solution.py:189
  443.1 4.6 fusion.129
  447.9 6.2 convolution_convert_fusion
  454.8 102.5 %reduce-scatter.9.cloned.1.call-done = f32[512,768]{1,0:T(8,128)} async-done(((f32[2048,768]{1,0:T(8,128)}), f32[512,768]{1,0:T(8,128)}) %reduce-scatter.9.cloned.1.call-update) | async-done | bytes 1572880 | tf_op jit(solution)/shard_map/reduce_scatter | solution.py:198
  559.9 60.3 %reduce-scatter.7.cloned.1.call-done = bf16[512,768]{1,0:T(8,128)(2,1)} async-done(((bf16[2048,768]{1,0:T(8,128)(2,1)}), bf16[512,768]{1,0:T(8,128)(2,1)}) %reduce-scatter.7.cloned.1.call-update) | async-done | bytes 786448 | tf_op jit(solution)/shard_map/reduce_scatter | solution.py:177
  629.0 7.1 fusion.132
  636.1 4.2 fusion.131
  640.3 49.2 %all-gather.17.cloned.1.call-done = bf16[2048,768]{1,0:T(8,128)(2,1)} async-done(((bf16[512,768]{1,0:T(8,128)(2,1)}), bf16[2048,768]{1,0:T(8,128)(2,1)}) %all-gather.17.cloned.1.call-update) | async-done | bytes 3145744 | tf_op jit(solution)/shard_map/all_gather | solution.py:207
  695.2 5.2 multiply_reduce_fusion
  700.6 10.7 fusion.23
  711.4 4.5 fusion.111
  717.4 5.2 all-gather.5
  725.4 6.5 all-gather.2
  732.4 5.7 multiply_add_fusion.2
  738.1 6.5 fusion.15
  744.6 4.5 fusion.17
  749.2 4.4 select_convert_fusion
  758.5 3.6 fusion.119
  762.1 3.4 copy.180
  773.0 3.6 fusion.118
  782.1 3.6 copy.179
  788.6 5.0 fusion.113
  799.1 4.9 bitcast_add_fusion
  818.1 6.0 convolution_convert_fusion.1
  824.2 127.9 %all-reduce.8.cloned.1.call-done = (f32[768,3,192]{0,2,1:T(8,128)}, f32[2,3,64,64]{3,2,1,0:T(8,128)}, f32[192,768]{1,0:T(8,128)}, f32[768,768]{1,0:T(8,128)}, f32[768,768]{1,0:T(8,128)}) async-done(((f32[768,3,192]{0,2,1:T(8,128)}, f32[2,3,64,64]{3,2,1,0:T(8,128)}, f32[192,768]{1,0:T(8,128)}, f32[768,768]{1,0:T(8,128)}, f32[768,768]{1,0:T(8,128)}), (f32[768,3,192]{0,2,1:T(8,128)}, ...) | async-done | bytes 7176208 | tf_op jit(solution)/shard_map/psum | solution.py:327
  952.2 62.8 %reduce-scatter.11.cloned.1.call-done = bf16[512,768]{1,0:T(8,128)(2,1)} async-done(((bf16[2048,768]{1,0:T(8,128)(2,1)}), bf16[512,768]{1,0:T(8,128)(2,1)}) %reduce-scatter.11.cloned.1.call-update) | async-done | bytes 786448 | tf_op jit(solution)/shard_map/reduce_scatter | solution.py:312
  1021.1 11.9 all-reduce.1
  1033.0 10.0 all-reduce.3
  1043.6 18.6 %all-reduce = (f32[768]{0:T(1024)}, f32[768]{0:T(1024)}, f32[768]{0:T(1024)}, f32[768]{0:T(1024)}, f32[768]{0:T(1024)}, /*index=5*/f32[768]{0:T(1024)}) all-reduce(f32[768]{0:T(1024)S(1)} %get-tuple-element.424, f32[768]{0:T(1024)S(1)} %get-tuple-element.425, ...), channel_id=1, replica_groups=mesh['dp'=2,'ctx'=4,'tp'=4] {'tp'}, use_global_device_ids=true, to_apply=%region_34.35 | all-reduce | flops 4608 | bytes 36864 | tf_op jit(solution)/shard_map/psum | solution.py:348
  1062.2 132.6 %all-reduce.10.cloned.1.call-done = (f32[768,3,192]{0,2,1:T(8,128)}, f32[2,3,64,64]{3,2,1,0:T(8,128)}, f32[192,768]{1,0:T(8,128)}, f32[768,768]{1,0:T(8,128)}, f32[768,768]{1,0:T(8,128)}) async-done(((f32[768,3,192]{0,2,1:T(8,128)}, f32[2,3,64,64]{3,2,1,0:T(8,128)}, f32[192,768]{1,0:T(8,128)}, f32[768,768]{1,0:T(8,128)}, f32[768,768]{1,0:T(8,128)}), (f32[768,3,192]{0,2,1:T(8,128)}, ...) | async-done | bytes 7176208 | tf_op jit(solution)/shard_map/psum | solution.py:326
  (351 shorter events, 150.2 us)
Async XLA Ops:
  7.2 422.0 %copy-start = (bf16[768,768]{1,0:T(8,128)(2,1)S(1)}, bf16[768,768]{1,0:T(8,128)(2,1)}, u32[]{:S(2)}) copy-start(bf16[768,768]{1,0:T(8,128)(2,1)} %param.34) | copy-start | bytes 3538948
  7.2 72.0 %all-gather.11.cloned.1.call-start = ((), (), s32[]{:S(2)}) async-start(), calls=%async_computation.4 | async-start | bytes 3932160 | tf_op jit(solution)/shard_map/all_gather | solution.py:95
  8.8 4.9 copy-start.72
  8.8 70.4 %copy-start.95 = (bf16[768,3,192]{0,2,1:T(8,128)(2,1)S(1)}, bf16[768,3,192]{0,2,1:T(8,128)(2,1)}, u32[]{:S(2)}) copy-start(bf16[768,3,192]{0,2,1:T(8,128)(2,1)} %param.24) | copy-start | bytes 2654212
  12.8 284.8 %reduce-scatter.5.cloned.1.call-start = ((), (), s32[]{:S(2)}) async-start(), calls=%async_computation.5 | async-start | bytes 7864320 | tf_op jit(solution)/shard_map/reduce_scatter | solution.py:160
  83.1 6.6 copy-start.31
  87.4 22.8 %copy-start.5 = (f32[2048,3,64]{0,2,1:T(8,128)}, f32[2048,3,64]{0,2,1:T(8,128)S(1)}, u32[]{:S(2)}) copy-start(f32[2048,3,64]{0,2,1:T(8,128)S(1)} %get-tuple-element.468) | copy-start | bytes 4718596
  117.1 9.8 copy-start.11
  117.1 9.8 copy-start.45
  121.4 5.5 copy-start.56
  161.4 7.7 copy-start.68
  161.4 5.7 copy-start.33
  161.4 5.7 copy-start.34
  169.0 7.3 copy-start.54
  169.1 7.3 copy-start.97
  171.6 4.7 copy-start.58
  171.6 4.8 copy-start.16
  188.0 177.6 %all-gather.13.cloned.1.call-start = ((), (), s32[]{:S(2)}) async-start(), calls=%async_computation.6 | async-start | bytes 3932160 | tf_op jit(solution)/shard_map/all_gather | solution.py:171
  301.4 127.8 %all-gather.15.cloned.1.call-start = ((), (), s32[]{:S(2)}) async-start(), calls=%async_computation.8 | async-start | bytes 3932160 | tf_op jit(solution)/shard_map/all_gather | solution.py:185
  302.0 255.3 %reduce-scatter.9.cloned.1.call-start = ((), (), s32[]{:S(2)}) async-start(), calls=%async_computation.9 | async-start | bytes 7864320 | tf_op jit(solution)/shard_map/reduce_scatter | solution.py:198
  429.2 13.9 %copy-start.94 = (bf16[768,768]{1,0:T(8,128)(2,1)S(1)}, bf16[768,768]{1,0:T(8,128)(2,1)}, u32[]{:S(2)}) copy-start(bf16[768,768]{1,0:T(8,128)(2,1)} %param.32) | copy-start | bytes 3538948
  447.7 172.5 %reduce-scatter.7.cloned.1.call-start = ((), (), s32[]{:S(2)}) async-start(), calls=%async_computation.7 | async-start | bytes 3932160 | tf_op jit(solution)/shard_map/reduce_scatter | solution.py:177
  454.1 235.3 %all-gather.17.cloned.1.call-start = ((), (), s32[]{:S(2)}) async-start(), calls=%async_computation.10 | async-start | bytes 3932160 | tf_op jit(solution)/shard_map/all_gather | solution.py:207
  454.8 105.1 %copy-start.76 = (f32[512]{0:T(512)S(1)}, f32[512]{0:T(512)}, u32[]{:S(2)}) copy-start(f32[512]{0:T(512)} %copy-done.75) | copy-start | bytes 6148
  559.9 64.7 %copy-start.29 = (bf16[512,768]{1,0:T(8,128)(2,1)S(1)}, bf16[512,768]{1,0:T(8,128)(2,1)}, u32[]{:S(2)}) copy-start(bf16[512,768]{1,0:T(8,128)(2,1)} %param.37) | copy-start | bytes 2359300
  625.8 326.3 %all-reduce.8.cloned.1.call-start = ((), (), s32[]{:S(2)}) async-start(), calls=%async_computation.12 | async-start | bytes 14548992 | tf_op jit(solution)/shard_map/psum | solution.py:327
  629.0 7.1 copy-start.93
  629.0 7.1 copy-start.100
  636.1 53.3 %copy-start.50 = (bf16[192,768]{1,0:T(8,128)(2,1)S(1)}, bf16[192,768]{1,0:T(8,128)(2,1)}, u32[]{:S(2)}) copy-start(bf16[192,768]{1,0:T(8,128)(2,1)} %param.28) | copy-start | bytes 884740
  692.5 7.9 copy-start.55
  692.5 7.9 copy-start.59
  695.2 5.3 copy-start.53
  695.2 5.4 copy-start.20
  695.2 5.4 copy-start.24
  700.6 10.8 copy-start.19
  715.9 9.5 copy-start.25
  725.4 7.0 copy-start.84
  732.4 5.7 copy-start.13
  738.1 6.5 copy-start.17
  788.6 5.0 copy-start.32
  793.6 5.6 copy-start.98
  817.0 198.1 %reduce-scatter.11.cloned.1.call-start = ((), (), s32[]{:S(2)}) async-start(), calls=%async_computation.11 | async-start | bytes 3932160 | tf_op jit(solution)/shard_map/reduce_scatter | solution.py:312
  824.1 370.7 %all-reduce.10.cloned.1.call-start = ((), (), s32[]{:S(2)}) async-start(), calls=%async_computation.13 | async-start | bytes 14548992 | tf_op jit(solution)/shard_map/psum | solution.py:326
  952.1 63.0 %copy-start.65 = (f32[768]{0:T(1024)S(1)}, f32[768]{0:T(1024)}, u32[]{:S(2)}) copy-start(f32[768]{0:T(1024)} %copy-done.64) | copy-start | bytes 9220
  952.1 63.0 %copy-start.67 = (f32[512]{0:T(512)S(1)}, f32[512]{0:T(512)}, u32[]{:S(2)}) copy-start(f32[512]{0:T(512)} %copy-done.66) | copy-start | bytes 6148
  952.1 64.8 %copy-start.74 = (f32[512]{0:T(512)S(1)}, f32[512]{0:T(512)}, u32[]{:S(2)}) copy-start(f32[512]{0:T(512)} %copy-done.73) | copy-start | bytes 6148
  952.1 64.8 %copy-start.71 = (f32[512]{0:T(512)S(1)}, f32[512]{0:T(512)}, u32[]{:S(2)}) copy-start(f32[512]{0:T(512)} %copy-done.70) | copy-start | bytes 6148
  952.2 66.8 %copy-start.15 = (f32[512,768]{1,0:T(8,128)S(1)}, f32[512,768]{1,0:T(8,128)}, u32[]{:S(2)}) copy-start(f32[512,768]{1,0:T(8,128)} %copy-done.14) | copy-start | bytes 4718596
  (63 other events, 169.8 us)
Sparse Core Ops, SparseCore 0:
  12.9 66.1 all-gather.10
  188.1 109.4 reduce-scatter.4
  301.5 64.0 all-gather.12
  367.0 62.1 all-gather.14
  447.8 109.3 reduce-scatter.8
  559.4 60.7 reduce-scatter.6
  625.9 63.5 all-gather.16
  817.1 134.9 all-reduce.7
  954.5 60.5 reduce-scatter.10
  1018.1 176.7 all-reduce.9
